TPU v7x, 32 devices: a whole 2x2x4 slice. The times are simulated.
32 devices in a mesh: dp: 4 (over y, x), ctx: 8 (over z, core).
Axes of the slice: x: 2, y: 2, z: 4, core: 2. Of those that a mesh axis runs over, the one named last changes fastest.
Arguments:
- inputs: bfloat16 [4, 2048, 4096], P('dp', 'ctx'), may hold values from -6 to 6
- query_weight: bfloat16 [4096, 128], P('dp'), may hold values from -0.09375 to 0.09375
- key_weight: bfloat16 [4096, 128], P('dp'), may hold values from -0.09375 to 0.09375
- value_weight: bfloat16 [4096, 2048], P('dp'), may hold values from -0.09375 to 0.09375
- lambda_weight: bfloat16 [4096, 320], P('dp'), may hold values from -0.09375 to 0.09375
- log_decay: float32 [4, 2048, 16], P('dp', 'ctx'), may hold values from -1 to 0, as said below
- norm_gain: float32 [2048], replicated, may hold values from 0.5 to 1.5
Outputs:
- outputs: bfloat16 [4, 2048, 2048], P('dp', 'ctx')
Inputs may be any that keep to these rules, and one draw needn't show every extreme that they name: `log_decay`: entries are not positive.
All inputs are finite; a program needn't handle non-finite values.
Results may differ from a plain program's by a relative error of at most 0.0072.
Values may be sent and summed in bfloat16 or wider, within the bound.
A program may use at most 128 MiB of HBM per device.

v0:
```python
import math
import jax
import jax.numpy as jnp
from jax import lax
from jax.sharding import PartitionSpec as P

HIGHEST = lax.Precision.HIGHEST


def from_partner(block, axis, stride):
    count = lax.axis_size(axis)
    route = []
    for low in range(count):
        high = low | 1 << stride
        if high != low and high < count:
            route += [(low, high), (high, low)]
    return lax.ppermute(block, axis, route)


def level_masks(length):
    depth = length.bit_length() - 1
    token_place = jnp.arange(length, dtype=jnp.int32)
    differ = jnp.bitwise_xor(token_place[:, None], token_place[None, :])
    level = jnp.zeros((length, length), jnp.int32)
    for power in range(depth):
        level = level + (differ >= 1 << power).astype(jnp.int32)
    levels = jnp.arange(depth + 1, dtype=jnp.int32)
    return (level[None, :, :] == levels[:, None, None]).astype(jnp.float32)


def block_terms(query_rows, key_rows, value_rows, lambdas, log_decay, masks):
    length, heads = log_decay.shape
    state_dim = query_rows.shape[1]
    head_dim = value_rows.shape[1] // heads
    inner = masks.shape[0]
    weights_all = lambdas.reshape(length, heads, -1)
    cumulative = jnp.cumsum(log_decay, axis=0)
    scores = lax.dot_general(
        query_rows, key_rows, (((1,), (1,)), ((), ())), preferred_element_type=jnp.float32
    ) / math.sqrt(state_dim)
    level_weight = jnp.einsum("lts,thl->hts", masks, weights_all[:, :, :inner], precision=HIGHEST)
    token_place = jnp.arange(length, dtype=jnp.int32)
    causal = token_place[:, None] >= token_place[None, :]
    spread = jnp.transpose(cumulative)
    distance = spread[:, :, None] - spread[:, None, :]
    decay = jnp.exp(jnp.where(causal[None], distance, -jnp.inf))
    mix = (level_weight * decay * scores[None]).astype(jnp.bfloat16)
    values = value_rows.reshape(length, heads, head_dim)
    near = jnp.einsum("hts,shd->thd", mix, values, preferred_element_type=jnp.float32)
    remain = jnp.exp(cumulative[-1][None, :] - cumulative)
    keyed = (key_rows.astype(jnp.float32)[:, None, :] * remain[:, :, None]).astype(jnp.bfloat16)
    state = jnp.einsum("chs,chd->hsd", keyed, values, preferred_element_type=jnp.float32)
    total = jnp.exp(cumulative[-1])
    return (near, state, total, cumulative, weights_all)


def finish(mixed, norm_gain):
    heads = mixed.shape[-2]
    mean_square = jnp.mean(mixed * mixed, axis=-1, keepdims=True)
    return (mixed * lax.rsqrt(mean_square + 1e-05) * norm_gain.reshape(heads, -1)).astype(
        jnp.bfloat16
    )


def make_fold(tokens):

    def accumulate(totals, pieces, start):
        return tuple(
            (jnp.dot(tokens, piece, preferred_element_type=jnp.float32) for piece in pieces)
        )

    return accumulate


def zeros_for(length, weights):
    return tuple((jnp.zeros((length, weight.shape[1]), jnp.float32) for weight in weights))


def per_device(inputs, query_weight, key_weight, value_weight, lambda_weight, log_decay, norm_gain):
    tokens = inputs[0]
    decays = log_decay[0]
    length = tokens.shape[0]
    accumulate = make_fold(tokens)
    query_sum, key_sum, value_sum, lambda_sum = accumulate(
        zeros_for(length, (query_weight, key_weight, value_weight, lambda_weight)),
        (
            lax.all_gather(query_weight, "dp", axis=0, tiled=True),
            lax.all_gather(key_weight, "dp", axis=0, tiled=True),
            lax.all_gather(value_weight, "dp", axis=0, tiled=True),
            lax.all_gather(lambda_weight, "dp", axis=0, tiled=True),
        ),
        jnp.int32(0),
    )
    query_rows = query_sum.astype(jnp.bfloat16)
    key_rows = key_sum.astype(jnp.bfloat16)
    value_rows = value_sum.astype(jnp.bfloat16)
    lambdas = jax.nn.softplus(lambda_sum)
    masks = level_masks(length)
    inner = masks.shape[0]
    scale = 1.0 / math.sqrt(query_rows.shape[1])
    near, state, total, cumulative, weights_all = block_terms(
        query_rows, key_rows, value_rows, lambdas, decays, masks
    )
    index = lax.axis_index("ctx")
    bits = lax.axis_size("ctx").bit_length() - 1
    block_state = state
    block_total = total
    carry_decay = jnp.ones_like(total)
    growth = jnp.exp(cumulative)
    mixed = near
    for level_bit in range(bits):
        other_state, other_total = from_partner((block_state, block_total), "ctx", level_bit)
        upper = (index >> level_bit & 1).astype(jnp.float32)
        carried = (carry_decay[:, None, None] * other_state).astype(jnp.bfloat16)
        reach = jnp.einsum("ts,hsd->thd", query_rows, carried, preferred_element_type=jnp.float32)
        factor = weights_all[:, :, inner + level_bit] * growth * (scale * upper)
        mixed = mixed + factor[..., None] * reach
        if level_bit + 1 < bits:
            block_state = jnp.where(
                upper > 0,
                block_total[:, None, None] * other_state + block_state,
                other_total[:, None, None] * block_state + other_state,
            )
            carry_decay = jnp.where(upper > 0, other_total * carry_decay, carry_decay)
            block_total = block_total * other_total
    return finish(mixed, norm_gain).reshape(1, length, -1)


def solution(mesh):
    return jax.shard_map(
        per_device,
        mesh=mesh,
        in_specs=(
            P("dp", "ctx", None),
            P("dp", None),
            P("dp", None),
            P("dp", None),
            P("dp", None),
            P("dp", "ctx", None),
            P(),
        ),
        out_specs=P("dp", "ctx", None),
        check_vma=False,
    )
```

profile of v0, /device:TPU:0, one launch (start us, length us, event | category | flops | bytes accessed | tf_op | source)
XLA Modules:
  0.0 352.5 jit_solution(18058356890450895991)
XLA Ops:
  6.5 0.7 all-gather.11.cloned.1.call-update
  7.3 0.7 all-gather.7.cloned.1.call-update
  8.1 0.7 all-gather.5.cloned.1.call-update
  9.9 28.5 %all-gather.11.cloned.1.call-done = bf16[4096,128]{1,0:T(8,128)(2,1)} async-done(((bf16[1024,128]{1,0:T(8,128)(2,1)}), bf16[4096,128]{1,0:T(8,128)(2,1)}) %all-gather.11.cloned.1.call-update) | async-done | bytes 1048592 | tf_op jit(solution)/shard_map/all_gather | solution.py:88
  38.4 1.9 fusion.21
  40.5 39.3 %all-gather.7.cloned.1.call-done = bf16[4096,320]{0,1:T(8,128)(2,1)} async-done(((bf16[1024,320]{0,1:T(8,128)(2,1)}), bf16[4096,320]{0,1:T(8,128)(2,1)}) %all-gather.7.cloned.1.call-update) | async-done | bytes 2621456 | tf_op jit(solution)/shard_map/all_gather | solution.py:90
  79.8 2.7 compare_select_fusion
  82.6 0.7 fusion.44
  83.4 155.6 %all-gather.5.cloned.1.call-done = bf16[4096,2048]{1,0:T(8,128)(2,1)} async-done(((bf16[1024,2048]{1,0:T(8,128)(2,1)}), bf16[4096,2048]{1,0:T(8,128)(2,1)}) %all-gather.5.cloned.1.call-update) | async-done | bytes 16777232 | tf_op jit(solution)/shard_map/all_gather | solution.py:89
  239.0 8.3 %fusion.15 = bf16[32,16,8,128]{3,2,1,0:T(8,128)(2,1)S(1)} fusion(bf16[4096,2048]{1,0:T(8,128)(2,1)} %all-gather.5.cloned.1.call-done, bf16[1,256,4096]{2,1,0:T(8,128)(2,1)S(1)} %copy-done), kind=kOutput, calls=%fused_computation.22 | convolution fusion | flops 4295491584 | bytes 19922944 | tf_op jit(solution)/shard_map/dot_general | solution.py:69
  247.3 1.0 copy-done.6
  249.4 0.8 convert_add_fusion
  250.2 1.4 collective-permute-done.1
  251.5 3.0 fusion.48
  254.6 1.5 collective-permute-start.2
  257.3 0.7 copy.39
  258.0 21.9 %collective-permute-done.3 = f32[16]{0:T(128)S(1)} collective-permute-done((f32[16]{0:T(128)S(1)}, f32[16]{0:T(128)S(1)}, u32[]{:S(2)}, u32[]{:S(2)}) %collective-permute-start.3) | collective-permute-done | bytes 96 | tf_op jit(solution)/shard_map/ppermute | solution.py:17
  280.5 1.9 fusion.18
  282.4 0.9 convolution_multiply_fusion
  283.3 2.5 copy.51
  285.9 2.9 multiply_convert_fusion.4
  288.8 2.4 collective-permute-start.4
  291.3 3.6 %fusion.1 = bf16[16,256,256]{2,0,1:T(8,128)(2,1)S(1)} fusion(f32[256,16,9]{2,1,0:T(8,128)S(1)} %copy-done.3, f32[256,256]{1,0:T(8,128)S(1)} %copy-done.9, f32[16,256]{1,0:T(8,128)S(1)} %copy-done.15, f32[16,256]{0,1:T(8,128)S(1)} %copy-done.11, s32[256,256]{1,0:T(8,128)S(1)} %copy-done.10, pred[256,256]{1,0:T(8,128)(4,1)S(1)} %copy-done.16), kind=kOutput, calls=%fused_computation.2 | convolution fusion | flops 119078912 | bytes 2867200 | tf_op jit(solution)/shard_map/lts,thl->hts/dot_general | solution.py:41
  294.9 2.3 fusion.12
  297.2 1.0 copy.45
  298.2 2.8 fusion.50
  301.3 1.8 fusion.51
  303.1 34.4 %collective-permute-done.4 = f32[16,128,128]{2,1,0:T(8,128)} collective-permute-done((f32[16,128,128]{2,1,0:T(8,128)}, f32[16,128,128]{2,1,0:T(8,128)}, u32[]{:S(2)}, u32[]{:S(2)}) %collective-permute-start.4) | collective-permute-done | bytes 1048608 | tf_op jit(solution)/shard_map/ppermute | solution.py:17
  337.5 1.4 multiply_convert_fusion.3
  339.7 1.1 copy-done.1
  340.8 3.3 multiply_reduce_fusion
  344.5 1.4 copy.49
  (83 shorter events, 5.7 us)
Async XLA Ops:
  6.5 31.9 %copy-start = (bf16[1,256,4096]{2,1,0:T(8,128)(2,1)S(1)}, bf16[1,256,4096]{2,1,0:T(8,128)(2,1)}, u32[]{:S(2)}) copy-start(bf16[1,256,4096]{2,1,0:T(8,128)(2,1)} %param.7) | copy-start | bytes 6291460
  6.5 31.9 %all-gather.11.cloned.1.call-start = ((), (), s32[]{:S(2)}) async-start(), calls=%async_computation.3 | async-start | bytes 1310720 | tf_op jit(solution)/shard_map/all_gather | solution.py:88
  7.3 72.6 %all-gather.7.cloned.1.call-start = ((), (), s32[]{:S(2)}) async-start(), calls=%async_computation.1 | async-start | bytes 3276800 | tf_op jit(solution)/shard_map/all_gather | solution.py:90
  8.0 231.0 %all-gather.5.cloned.1.call-start = ((), (), s32[]{:S(2)}) async-start(), calls=%async_computation | async-start | bytes 20971520 | tf_op jit(solution)/shard_map/all_gather | solution.py:89
  8.8 271.7 %all-gather.9.cloned.1.call-start = ((), (), s32[]{:S(2)}) async-start(), calls=%async_computation.2 | async-start | bytes 1310720 | tf_op jit(solution)/shard_map/all_gather | solution.py:87
  9.7 247.6 %copy-start.14 = (f32[16,256]{1,0:T(8,128)}, f32[16,256]{1,0:T(8,128)S(1)}, u32[]{:S(2)}) copy-start(f32[16,256]{1,0:T(8,128)S(1)} %get-tuple-element.16) | copy-start | bytes 49156
  82.6 164.7 %copy-start.5 = (f32[256,16,20]{0,2,1:T(8,128)}, f32[256,16,20]{0,2,1:T(8,128)S(1)}, u32[]{:S(2)}) copy-start(f32[256,16,20]{0,2,1:T(8,128)S(1)} %reshape.113) | copy-start | bytes 983044
  247.2 1.0 copy-start.6
  248.7 2.9 copy-start.8
  248.7 2.9 collective-permute-start
  248.8 2.7 collective-permute-start.1
  251.5 5.7 %copy-start.20 = (f32[16]{0:T(128)}, f32[16]{0:T(128)S(1)}, u32[]{:S(2)}) copy-start(f32[16]{0:T(128)S(1)} %collective-permute-done.1) | copy-start | bytes 196
  254.6 31.3 %collective-permute-start.2 = (f32[16,128,128]{2,1,0:T(8,128)S(1)}, f32[16,128,128]{2,1,0:T(8,128)}, u32[]{:S(2)}, u32[]{:S(2)}) collective-permute-start(f32[16,128,128]{2,1,0:T(8,128)S(1)} %get-tuple-element.10), channel_id=1, source_target_pairs={{0,2},{2,0},{1,3},{3,1},{4,6},{6,4},{5,7},{7,5},{8,10},{10,8},{9,1... | collective-permute-start | bytes 3145736 | tf_op jit(solution)/shard_map/ppermute | solution.py:17
  256.7 23.8 %copy-start.24 = (f32[16]{0:T(128)}, f32[16]{0:T(128)S(1)}, u32[]{:S(2)}) copy-start(f32[16]{0:T(128)S(1)} %exponential_multiply_fusion) | copy-start | bytes 196
  256.7 23.2 %collective-permute-start.3 = (f32[16]{0:T(128)S(1)}, f32[16]{0:T(128)S(1)}, u32[]{:S(2)}, u32[]{:S(2)}) collective-permute-start(f32[16]{0:T(128)S(1)} %exponential_multiply_fusion), channel_id=1, source_target_pairs={{0,2},{2,0},{1,3},{3,1},{4,6},{6,4},{5,7},{7,5},{8,10},{10,8},{9,1... | collective-permute-start | bytes 200 | tf_op jit(solution)/shard_map/ppermute | solution.py:17
  258.0 25.3 %slice-start = ((f32[256,16,20]{0,2,1:T(8,128)}), f32[256,16,9]{0,2,1:T(8,128)S(1)}, s32[]{:S(2)}) async-start(f32[256,16,20]{0,2,1:T(8,128)} %copy-done.5), calls=%async_computation.4 | async-start | bytes 524288 | tf_op jit(solution)/shard_map/slice | solution.py:41
  283.3 2.6 copy-start.22
  283.3 2.6 copy-start.23
  283.3 2.6 copy-start.25
  285.9 5.4 %copy-start.3 = (f32[256,16,9]{2,1,0:T(8,128)S(1)}, f32[256,16,9]{2,1,0:T(8,128)}, u32[]{:S(2)}) copy-start(f32[256,16,9]{2,1,0:T(8,128)} %copy.51) | copy-start | bytes 442372
  285.9 5.4 %copy-start.9 = (f32[256,256]{1,0:T(8,128)S(1)}, f32[256,256]{1,0:T(8,128)}, u32[]{:S(2)}) copy-start(f32[256,256]{1,0:T(8,128)} %convolution_multiply_fusion) | copy-start | bytes 786436
  285.9 5.4 %copy-start.10 = (s32[256,256]{1,0:T(8,128)S(1)}, s32[256,256]{1,0:T(8,128)}, u32[]{:S(2)}) copy-start(s32[256,256]{1,0:T(8,128)} %convert_add_fusion) | copy-start | bytes 786436
  285.9 5.4 %copy-start.11 = (f32[16,256]{0,1:T(8,128)S(1)}, f32[16,256]{0,1:T(8,128)}, u32[]{:S(2)}) copy-start(f32[16,256]{0,1:T(8,128)} %copy.39) | copy-start | bytes 49156
  285.9 5.4 %copy-start.15 = (f32[16,256]{1,0:T(8,128)S(1)}, f32[16,256]{1,0:T(8,128)}, u32[]{:S(2)}) copy-start(f32[16,256]{1,0:T(8,128)} %copy-done.14) | copy-start | bytes 49156
  285.9 5.4 %copy-start.16 = (pred[256,256]{1,0:T(8,128)(4,1)S(1)}, pred[256,256]{1,0:T(8,128)(4,1)}, u32[]{:S(2)}) copy-start(pred[256,256]{1,0:T(8,128)(4,1)} %iota_compare_fusion.4) | copy-start | bytes 196612
  288.8 6.1 %copy-start.7 = (bf16[32,16,8,128]{3,2,1,0:T(8,128)(2,1)S(1)}, bf16[32,16,8,128]{3,2,1,0:T(8,128)(2,1)}, u32[]{:S(2)}) copy-start(bf16[32,16,8,128]{3,2,1,0:T(8,128)(2,1)} %copy-done.6) | copy-start | bytes 3145732
  288.8 48.7 %collective-permute-start.4 = (f32[16,128,128]{2,1,0:T(8,128)}, f32[16,128,128]{2,1,0:T(8,128)}, u32[]{:S(2)}, u32[]{:S(2)}) collective-permute-start(f32[16,128,128]{2,1,0:T(8,128)} %get-tuple-element.12), channel_id=1, source_target_pairs={{0,4},{4,0},{1,5},{5,1},{2,6},{6,2},{3,7},{7,3},{8,12},{12,8},{9,1... | collective-permute-start | bytes 3145736 | tf_op jit(solution)/shard_map/ppermute | solution.py:17
  294.9 2.3 copy-start.4
  297.2 3.8 %copy-start.2 = (bf16[16,128,128]{2,1,0:T(8,128)(2,1)S(1)}, bf16[16,128,128]{2,1,0:T(8,128)(2,1)}, u32[]{:S(2)}) copy-start(bf16[16,128,128]{2,1,0:T(8,128)(2,1)} %get-tuple-element.11) | copy-start | bytes 1572868
  301.0 36.5 %copy-start.19 = (f32[16]{0:T(128)S(1)}, f32[16]{0:T(128)}, u32[]{:S(2)}) copy-start(f32[16]{0:T(128)} %get-tuple-element.7) | copy-start | bytes 196
  339.2 1.6 copy-start.1
  340.8 3.3 copy-start.18
  (4 other events, 2.9 us)
Sparse Core Ops, SparseCore 0:
  9.2 29.2 all-gather.10
  40.3 39.4 all-gather.6
  81.7 157.2 all-gather.4
  248.9 26.6 all-gather.8
where the time goes:
time: 353 us; the launch traced here: 352 us
  waiting for transfers between devices  283 us (80%)
  matrix products  27.1 us (8%)
  other arithmetic  14.4 us (4%)
  between operations  13.5 us (4%)
  local copies, waits for them, and re-layouts  8.98 us (3%)
  starting transfers between devices  5.18 us (1%)
    all_gather x1, waiting for transfers between devices, per_device(): lax.all_gather(value_weight, 'dp', axis=0, tiled=True)  156 us
    ppermute x5, waiting for transfers between devices, from_partner(): return lax.ppermute(block, axis, route)  57.7 us
    all_gather x1, waiting for transfers between devices, per_device(): lax.all_gather(lambda_weight, 'dp', axis=0, tiled=True)  39.3 us
    all_gather x1, waiting for transfers between devices, per_device(): lax.all_gather(key_weight, 'dp', axis=0, tiled=True)  28.5 us
    dot_general x4, matrix products, accumulate(): jnp.dot(tokens, piece, preferred_element_type=jnp.float32)  14.8 us
    convert_element_type x3, other arithmetic, per_device(): carried = (carry_decay[:, None, None] * other_state).astype(jnp.bfloat16)  7.3 us
  transfers between devices with their start and end apart: 9, of which 6 were waited for; matrix products, arithmetic and copies ran while one was open for 8% of the time, Pallas kernels for 0%

commit v1 on v0

--- a/solution.py
+++ b/solution.py
@@ -5,6 +5,17 @@
 from jax.sharding import PartitionSpec as P
 
 HIGHEST = lax.Precision.HIGHEST
+
+
+def ring_gather(x, axis, dim):
+    ways = lax.axis_size(axis)
+    pieces = [x]
+    for far in range(1, ways):
+        pieces.append(
+            lax.ppermute(pieces[far - 1], axis, [(d, (d - 1) % ways) for d in range(ways)])
+        )
+    line = jnp.concatenate(pieces, axis=dim)
+    return jnp.roll(line, lax.axis_index(axis) * x.shape[dim], axis=dim)
 
 
 def from_partner(block, axis, stride):
@@ -85,7 +96,7 @@
         zeros_for(length, (query_weight, key_weight, value_weight, lambda_weight)),
         (
             lax.all_gather(query_weight, "dp", axis=0, tiled=True),
-            lax.all_gather(key_weight, "dp", axis=0, tiled=True),
+            ring_gather(key_weight, "dp", 0),
             lax.all_gather(value_weight, "dp", axis=0, tiled=True),
             lax.all_gather(lambda_weight, "dp", axis=0, tiled=True),
         ),

time: 353 us -> 332 us (0.941)
  waiting for transfers between devices: 283 us -> 246 us
  starting transfers between devices: 5.18 us -> 15.8 us
  local copies, waits for them, and re-layouts: 8.98 us -> 14.8 us
    all_gather x1 -> x0, waiting for transfers between devices: 28.5 us -> none  [per_device(): lax.all_gather(key_weight, 'dp', axis=0, tiled=True)]
    all_gather x1, waiting for transfers between devices: 39.3 us -> 13.4 us  [per_device(): lax.all_gather(lambda_weight, 'dp', axis=0, tiled=True)]
    ppermute x0 -> x3, waiting for transfers between devices: none -> 17.9 us  [ring_gather(): lax.ppermute(pieces[far - 1], axis, [(d, (d - 1) % ways) for d in range(w...]
    ppermute x0 -> x3, starting transfers between devices: none -> 10.7 us  [ring_gather(): lax.ppermute(pieces[far - 1], axis, [(d, (d - 1) % ways) for d in range(w...]
    unnamed x53 -> x62, local copies, waits for them, and re-layouts: 4.71 us -> 9.9 us
  transfers between devices with their start and end apart: 9 -> 11, of which waited for: 6 -> 8; matrix products, arithmetic and copies ran while one was open for 8% -> 11% of each run, Pallas kernels for 0% -> 0%
where the time goes in v1:
time: 332 us
  waiting for transfers between devices  246 us (74%)
  matrix products  27.1 us (8%)
  starting transfers between devices  15.8 us (5%)
  local copies, waits for them, and re-layouts  14.8 us (4%)
  other arithmetic  14.4 us (4%)
  between operations  13.5 us (4%)
    all_gather x1, waiting for transfers between devices, per_device(): lax.all_gather(value_weight, 'dp', axis=0, tiled=True)  156 us
    ppermute x5, waiting for transfers between devices, from_partner(): return lax.ppermute(block, axis, route)  57.8 us
    ppermute x3, waiting for transfers between devices, ring_gather(): lax.ppermute(pieces[far - 1], axis, [(d, (d - 1) % ways) for d in range(w...  17.9 us
    dot_general x4, matrix products, accumulate(): jnp.dot(tokens, piece, preferred_element_type=jnp.float32)  14.9 us
    all_gather x1, waiting for transfers between devices, per_device(): lax.all_gather(lambda_weight, 'dp', axis=0, tiled=True)  13.4 us
    ppermute x3, starting transfers between devices, ring_gather(): lax.ppermute(pieces[far - 1], axis, [(d, (d - 1) % ways) for d in range(w...  10.7 us
    unnamed x62, local copies, waits for them, and re-layouts  9.9 us
    convert_element_type x3, other arithmetic, per_device(): carried = (carry_decay[:, None, None] * other_state).astype(jnp.bfloat16)  7.29 us
  transfers between devices with their start and end apart: 11, of which 8 were waited for; matrix products, arithmetic and copies ran while one was open for 11% of the time, Pallas kernels for 0%

profile of v1, /device:TPU:0, one launch (start us, length us, event | category | flops | bytes accessed | tf_op | source)
XLA Modules:
  0.0 331.6 jit_solution(5717390410386847655)
XLA Ops:
  8.2 3.9 %collective-permute-start = (bf16[1024,128]{1,0:T(8,128)(2,1)S(1)}, bf16[1024,128]{1,0:T(8,128)(2,1)S(1)}, u32[]{:S(2)}, u32[]{:S(2)}) collective-permute-start(bf16[1024,128]{1,0:T(8,128)(2,1)S(1)} %copy-done.9), channel_id=1, source_target_pairs={{0,24},{8,0},{16,8},{24,16},{1,25},{9,1},{17,9},{25,17},{2,26},{10... | collective-permute-start | bytes 786440 | tf_op jit(solution)/shard_map/ppermute | solution.py:15
  13.4 4.3 %collective-permute-done = bf16[1024,128]{1,0:T(8,128)(2,1)S(1)} collective-permute-done((bf16[1024,128]{1,0:T(8,128)(2,1)S(1)}, bf16[1024,128]{1,0:T(8,128)(2,1)S(1)}, u32[]{:S(2)}, u32[]{:S(2)}) %collective-permute-start) | collective-permute-done | bytes 262176 | tf_op jit(solution)/shard_map/ppermute | solution.py:15
  17.7 3.4 %collective-permute-start.1 = (bf16[1024,128]{1,0:T(8,128)(2,1)S(1)}, bf16[1024,128]{1,0:T(8,128)(2,1)S(1)}, u32[]{:S(2)}, u32[]{:S(2)}) collective-permute-start(bf16[1024,128]{1,0:T(8,128)(2,1)S(1)} %collective-permute-done), channel_id=1, source_target_pairs={{0,24},{8,0},{16,8},{24,16},{1,25},{9,1},{17,9},{25,17},{2,26},{10... | collective-permute-start | bytes 786440 | tf_op jit(solution)/shard_map/ppermute | solution.py:15
  21.4 11.3 %collective-permute-done.1 = bf16[1024,128]{1,0:T(8,128)(2,1)S(1)} collective-permute-done((bf16[1024,128]{1,0:T(8,128)(2,1)S(1)}, bf16[1024,128]{1,0:T(8,128)(2,1)S(1)}, u32[]{:S(2)}, u32[]{:S(2)}) %collective-permute-start.1) | collective-permute-done | bytes 262176 | tf_op jit(solution)/shard_map/ppermute | solution.py:15
  32.7 3.4 %collective-permute-start.2 = (bf16[1024,128]{1,0:T(8,128)(2,1)S(1)}, bf16[1024,128]{1,0:T(8,128)(2,1)S(1)}, u32[]{:S(2)}, u32[]{:S(2)}) collective-permute-start(bf16[1024,128]{1,0:T(8,128)(2,1)S(1)} %collective-permute-done.1), channel_id=1, source_target_pairs={{0,24},{8,0},{16,8},{24,16},{1,25},{9,1},{17,9},{25,17},{2,26},{10... | collective-permute-start | bytes 786440 | tf_op jit(solution)/shard_map/ppermute | solution.py:15
  37.7 2.3 collective-permute-done.2
  43.6 2.1 fusion.21
  45.7 13.4 %all-gather.6.cloned.1.call-done = bf16[4096,320]{0,1:T(8,128)(2,1)} async-done(((bf16[1024,320]{0,1:T(8,128)(2,1)}), bf16[4096,320]{0,1:T(8,128)(2,1)}) %all-gather.6.cloned.1.call-update) | async-done | bytes 2621456 | tf_op jit(solution)/shard_map/all_gather | solution.py:101
  59.0 2.7 compare_select_fusion
  62.6 155.5 %all-gather.4.cloned.1.call-done = bf16[4096,2048]{1,0:T(8,128)(2,1)} async-done(((bf16[1024,2048]{1,0:T(8,128)(2,1)}), bf16[4096,2048]{1,0:T(8,128)(2,1)}) %all-gather.4.cloned.1.call-update) | async-done | bytes 16777232 | tf_op jit(solution)/shard_map/all_gather | solution.py:100
  218.1 8.3 %fusion.15 = bf16[32,16,8,128]{3,2,1,0:T(8,128)(2,1)S(1)} fusion(bf16[4096,2048]{1,0:T(8,128)(2,1)} %all-gather.4.cloned.1.call-done, bf16[1,256,4096]{2,1,0:T(8,128)(2,1)S(1)} %copy-done), kind=kOutput, calls=%fused_computation.22 | convolution fusion | flops 4295491584 | bytes 19922944 | tf_op jit(solution)/shard_map/dot_general | solution.py:80
  226.4 1.0 copy-done.6
  228.5 0.8 convert_add_fusion
  229.3 1.4 collective-permute-done.4
  230.7 3.0 fusion.50
  233.7 1.5 collective-permute-start.5
  237.1 21.9 %collective-permute-done.6 = f32[16]{0:T(128)S(1)} collective-permute-done((f32[16]{0:T(128)S(1)}, f32[16]{0:T(128)S(1)}, u32[]{:S(2)}, u32[]{:S(2)}) %collective-permute-start.6) | collective-permute-done | bytes 96 | tf_op jit(solution)/shard_map/ppermute | solution.py:28
  259.6 1.9 fusion.18
  261.5 0.9 convolution_multiply_fusion
  262.4 2.5 copy.48
  265.0 2.9 multiply_convert_fusion.4
  267.9 2.4 collective-permute-start.7
  270.4 3.4 %fusion.1 = bf16[16,256,256]{2,0,1:T(8,128)(2,1)S(1)} fusion(f32[256,16,9]{2,1,0:T(8,128)S(1)} %copy-done.3, f32[256,256]{1,0:T(8,128)S(1)} %copy-done.10, f32[16,256]{1,0:T(8,128)S(1)} %copy-done.16, f32[16,256]{0,1:T(8,128)S(1)} %copy-done.12, s32[256,256]{1,0:T(8,128)S(1)} %copy-done.11, pred[256,256]{1,0:T(8,128)(4,1)S(1)} %copy-done.17), kind=kOutput, calls=%fused_computation.2 | convolution fusion | flops 119078912 | bytes 2867200 | tf_op jit(solution)/shard_map/lts,thl->hts/dot_general | solution.py:52
  273.8 2.3 fusion.12
  276.1 1.0 copy.42
  277.2 2.8 fusion.52
  280.2 1.8 fusion.53
  282.1 34.6 %collective-permute-done.7 = f32[16,128,128]{2,1,0:T(8,128)} collective-permute-done((f32[16,128,128]{2,1,0:T(8,128)}, f32[16,128,128]{2,1,0:T(8,128)}, u32[]{:S(2)}, u32[]{:S(2)}) %collective-permute-start.7) | collective-permute-done | bytes 1048608 | tf_op jit(solution)/shard_map/ppermute | solution.py:28
  316.6 1.4 multiply_convert_fusion.3
  318.8 1.1 copy-done.1
  319.9 3.3 %multiply_reduce_fusion = (f32[256,16]{0,1:T(8,128)S(1)}, f32[256,16,128]{0,2,1:T(8,128)S(1)}) fusion(f32[256,16]{0,1:T(8,128)S(1)} %copy-done.14, f32[256,16]{0,1:T(8,128)S(1)} %copy-done.13, f32[256,16]{0,1:T(8,128)S(1)} %get-tuple-element.18, f32[16,128,256]{2,1,0:T(8,128)S(1)} %copy-done.1, f32[256,2048]{0,1:S(1)} %fusion.54, f32[256,2048]{0,1} %fusion.53, ...), kind=kLoop, calls=%fused_computation.19 | loop fusion | flops 4190208 | bytes 10551296 | tf_op jit(solution)/shard_map/reduce_sum | solution.py:70
  323.6 1.4 copy.46
  (96 shorter events, 14.3 us)
Async XLA Ops:
  6.5 37.0 %copy-start = (bf16[1,256,4096]{2,1,0:T(8,128)(2,1)S(1)}, bf16[1,256,4096]{2,1,0:T(8,128)(2,1)}, u32[]{:S(2)}) copy-start(bf16[1,256,4096]{2,1,0:T(8,128)(2,1)} %param.7) | copy-start | bytes 6291460
  6.5 52.5 %all-gather.6.cloned.1.call-start = ((), (), s32[]{:S(2)}) async-start(), calls=%async_computation.1 | async-start | bytes 3276800 | tf_op jit(solution)/shard_map/all_gather | solution.py:101
  7.3 4.9 %copy-start.18 = (f32[1,256,16]{1,2,0:T(8,128)S(1)}, f32[1,256,16]{1,2,0:T(8,128)}, u32[]{:S(2)}) copy-start(f32[1,256,16]{1,2,0:T(8,128)} %param.12) | copy-start | bytes 49156
  7.3 210.8 %all-gather.4.cloned.1.call-start = ((), (), s32[]{:S(2)}) async-start(), calls=%async_computation | async-start | bytes 20971520 | tf_op jit(solution)/shard_map/all_gather | solution.py:100
  8.0 251.6 %all-gather.8.cloned.1.call-start = ((), (), s32[]{:S(2)}) async-start(), calls=%async_computation.2 | async-start | bytes 1310720 | tf_op jit(solution)/shard_map/all_gather | solution.py:98
  8.2 9.5 %collective-permute-start = (bf16[1024,128]{1,0:T(8,128)(2,1)S(1)}, bf16[1024,128]{1,0:T(8,128)(2,1)S(1)}, u32[]{:S(2)}, u32[]{:S(2)}) collective-permute-start(bf16[1024,128]{1,0:T(8,128)(2,1)S(1)} %copy-done.9), channel_id=1, source_target_pairs={{0,24},{8,0},{16,8},{24,16},{1,25},{9,1},{17,9},{25,17},{2,26},{10... | collective-permute-start | bytes 786440 | tf_op jit(solution)/shard_map/ppermute | solution.py:15
  17.7 15.0 %collective-permute-start.1 = (bf16[1024,128]{1,0:T(8,128)(2,1)S(1)}, bf16[1024,128]{1,0:T(8,128)(2,1)S(1)}, u32[]{:S(2)}, u32[]{:S(2)}) collective-permute-start(bf16[1024,128]{1,0:T(8,128)(2,1)S(1)} %collective-permute-done), channel_id=1, source_target_pairs={{0,24},{8,0},{16,8},{24,16},{1,25},{9,1},{17,9},{25,17},{2,26},{10... | collective-permute-start | bytes 786440 | tf_op jit(solution)/shard_map/ppermute | solution.py:15
  21.4 215.0 %copy-start.15 = (f32[16,256]{1,0:T(8,128)}, f32[16,256]{1,0:T(8,128)S(1)}, u32[]{:S(2)}) copy-start(f32[16,256]{1,0:T(8,128)S(1)} %get-tuple-element.16) | copy-start | bytes 49156
  32.7 7.3 %collective-permute-start.2 = (bf16[1024,128]{1,0:T(8,128)(2,1)S(1)}, bf16[1024,128]{1,0:T(8,128)(2,1)S(1)}, u32[]{:S(2)}, u32[]{:S(2)}) collective-permute-start(bf16[1024,128]{1,0:T(8,128)(2,1)S(1)} %collective-permute-done.1), channel_id=1, source_target_pairs={{0,24},{8,0},{16,8},{24,16},{1,25},{9,1},{17,9},{25,17},{2,26},{10... | collective-permute-start | bytes 786440 | tf_op jit(solution)/shard_map/ppermute | solution.py:15
  61.8 164.6 %copy-start.5 = (f32[256,16,20]{0,2,1:T(8,128)}, f32[256,16,20]{0,2,1:T(8,128)S(1)}, u32[]{:S(2)}) copy-start(f32[256,16,20]{0,2,1:T(8,128)S(1)} %reshape.113) | copy-start | bytes 983044
  227.8 2.9 copy-start.8
  227.8 2.9 collective-permute-start.3
  227.9 2.7 collective-permute-start.4
  230.7 5.7 %copy-start.21 = (f32[16]{0:T(128)}, f32[16]{0:T(128)S(1)}, u32[]{:S(2)}) copy-start(f32[16]{0:T(128)S(1)} %collective-permute-done.4) | copy-start | bytes 196
  233.7 31.3 %collective-permute-start.5 = (f32[16,128,128]{2,1,0:T(8,128)S(1)}, f32[16,128,128]{2,1,0:T(8,128)}, u32[]{:S(2)}, u32[]{:S(2)}) collective-permute-start(f32[16,128,128]{2,1,0:T(8,128)S(1)} %get-tuple-element.10), channel_id=1, source_target_pairs={{0,2},{2,0},{1,3},{3,1},{4,6},{6,4},{5,7},{7,5},{8,10},{10,8},{9,1... | collective-permute-start | bytes 3145736 | tf_op jit(solution)/shard_map/ppermute | solution.py:28
  235.8 23.8 %copy-start.25 = (f32[16]{0:T(128)}, f32[16]{0:T(128)S(1)}, u32[]{:S(2)}) copy-start(f32[16]{0:T(128)S(1)} %exponential_multiply_fusion) | copy-start | bytes 196
  235.8 23.2 %collective-permute-start.6 = (f32[16]{0:T(128)S(1)}, f32[16]{0:T(128)S(1)}, u32[]{:S(2)}, u32[]{:S(2)}) collective-permute-start(f32[16]{0:T(128)S(1)} %exponential_multiply_fusion), channel_id=1, source_target_pairs={{0,2},{2,0},{1,3},{3,1},{4,6},{6,4},{5,7},{7,5},{8,10},{10,8},{9,1... | collective-permute-start | bytes 200 | tf_op jit(solution)/shard_map/ppermute | solution.py:28
  237.1 25.3 %slice-start = ((f32[256,16,20]{0,2,1:T(8,128)}), f32[256,16,9]{0,2,1:T(8,128)S(1)}, s32[]{:S(2)}) async-start(f32[256,16,20]{0,2,1:T(8,128)} %copy-done.5), calls=%async_computation.3 | async-start | bytes 524288 | tf_op jit(solution)/shard_map/slice | solution.py:52
  262.4 2.6 copy-start.23
  262.4 2.6 copy-start.24
  262.4 2.6 copy-start.26
  265.0 5.4 %copy-start.3 = (f32[256,16,9]{2,1,0:T(8,128)S(1)}, f32[256,16,9]{2,1,0:T(8,128)}, u32[]{:S(2)}) copy-start(f32[256,16,9]{2,1,0:T(8,128)} %copy.48) | copy-start | bytes 442372
  265.0 5.4 %copy-start.10 = (f32[256,256]{1,0:T(8,128)S(1)}, f32[256,256]{1,0:T(8,128)}, u32[]{:S(2)}) copy-start(f32[256,256]{1,0:T(8,128)} %convolution_multiply_fusion) | copy-start | bytes 786436
  265.0 5.4 %copy-start.11 = (s32[256,256]{1,0:T(8,128)S(1)}, s32[256,256]{1,0:T(8,128)}, u32[]{:S(2)}) copy-start(s32[256,256]{1,0:T(8,128)} %convert_add_fusion) | copy-start | bytes 786436
  265.0 5.4 %copy-start.12 = (f32[16,256]{0,1:T(8,128)S(1)}, f32[16,256]{0,1:T(8,128)}, u32[]{:S(2)}) copy-start(f32[16,256]{0,1:T(8,128)} %copy.37) | copy-start | bytes 49156
  265.0 5.4 %copy-start.16 = (f32[16,256]{1,0:T(8,128)S(1)}, f32[16,256]{1,0:T(8,128)}, u32[]{:S(2)}) copy-start(f32[16,256]{1,0:T(8,128)} %copy-done.15) | copy-start | bytes 49156
  265.0 5.4 %copy-start.17 = (pred[256,256]{1,0:T(8,128)(4,1)S(1)}, pred[256,256]{1,0:T(8,128)(4,1)}, u32[]{:S(2)}) copy-start(pred[256,256]{1,0:T(8,128)(4,1)} %iota_compare_fusion.4) | copy-start | bytes 196612
  267.9 5.9 %copy-start.7 = (bf16[32,16,8,128]{3,2,1,0:T(8,128)(2,1)S(1)}, bf16[32,16,8,128]{3,2,1,0:T(8,128)(2,1)}, u32[]{:S(2)}) copy-start(bf16[32,16,8,128]{3,2,1,0:T(8,128)(2,1)} %copy-done.6) | copy-start | bytes 3145732
  267.9 48.7 %collective-permute-start.7 = (f32[16,128,128]{2,1,0:T(8,128)}, f32[16,128,128]{2,1,0:T(8,128)}, u32[]{:S(2)}, u32[]{:S(2)}) collective-permute-start(f32[16,128,128]{2,1,0:T(8,128)} %get-tuple-element.12), channel_id=1, source_target_pairs={{0,4},{4,0},{1,5},{5,1},{2,6},{6,2},{3,7},{7,3},{8,12},{12,8},{9,1... | collective-permute-start | bytes 3145736 | tf_op jit(solution)/shard_map/ppermute | solution.py:28
  276.1 3.8 %copy-start.2 = (bf16[16,128,128]{2,1,0:T(8,128)(2,1)S(1)}, bf16[16,128,128]{2,1,0:T(8,128)(2,1)}, u32[]{:S(2)}) copy-start(bf16[16,128,128]{2,1,0:T(8,128)(2,1)} %get-tuple-element.11) | copy-start | bytes 1572868
  280.0 36.7 %copy-start.20 = (f32[16]{0:T(128)S(1)}, f32[16]{0:T(128)}, u32[]{:S(2)}) copy-start(f32[16]{0:T(128)} %get-tuple-element.7) | copy-start | bytes 196
  319.9 3.3 %copy-start.19 = (f32[2048]{0:T(1024)S(1)}, f32[2048]{0:T(1024)}, u32[]{:S(2)}) copy-start(f32[2048]{0:T(1024)} %param.13) | copy-start | bytes 24580
  (7 other events, 7.9 us)
Sparse Core Ops, SparseCore 0:
  9.2 49.8 all-gather.5
  60.9 157.1 all-gather.3
  228.0 26.6 all-gather.7
